TPU v7x, 32 devices: a whole 2x2x4 slice. The times are simulated.
32 devices in a mesh: seq: 8 (over y, x, core), red: 4 (over z).
Axes of the slice: x: 2, y: 2, z: 4, core: 2. Of those that a mesh axis runs over, the one named last changes fastest.
Arguments:
- token_ids: int32 [1024], P('seq'), may hold values from 0 to 511
- embedding: bfloat16 [512, 4096], P(None, 'red'), may hold values from -6 to 6
- proj_weight: bfloat16 [4096, 3, 4, 256], P('red', None, None, 'seq'), may hold values from -0.09375 to 0.09375
- filters: float32 [1024, 1024], P('seq', 'red'), may hold values from -1 to 1
- cotangent: float32 [1024, 1024], P('seq', 'red'), may hold values from -6 to 6
Outputs:
- output: float32 [1024, 1024], P('seq', 'red')
- filter_grad: float32 [1024, 1024], P('seq', 'red')
- branch_grads: bfloat16 [1024, 3, 1024], P('seq', None, 'red')
- weight_grad: float32 [4096, 3, 4, 256], P('red', None, None, 'seq')
All inputs are finite; a program needn't handle non-finite values.
Results may differ from a plain program's by a relative error of at most 0.0029.
Values sent between devices are 32-bit elements; how exact they have to be, the bound alone decides.
A program may use at most 64 MiB of HBM per device.

v0:
```python
import math

import jax
import jax.numpy as jnp
from jax import lax
from jax.sharding import PartitionSpec as P

precise_mode = lax.Precision.HIGHEST


def angles(numbers, modulus, direction):
    phase = (numbers % modulus).astype(jnp.float32) * (direction * 2.0 * math.pi / modulus)
    return (jnp.cos(phase), jnp.sin(phase))


def rotate(real_part, imag_part, cosine, sine_part):
    return (real_part * cosine - imag_part * sine_part, real_part * sine_part + imag_part * cosine)


def complex_einsum(formula, matrix, values):
    mat_real, mat_imag = matrix
    val_real, val_imag = values
    real_out = jnp.einsum(formula, mat_real, val_real, precision=precise_mode) - jnp.einsum(
        formula, mat_imag, val_imag, precision=precise_mode
    )
    imag_out = jnp.einsum(formula, mat_real, val_imag, precision=precise_mode) + jnp.einsum(
        formula, mat_imag, val_real, precision=precise_mode
    )
    return (real_out, imag_out)


def factors(length_total):
    first_factor = 1
    for candidate in range(1, math.isqrt(length_total) + 1):
        if length_total % candidate == 0:
            first_factor = candidate
    return (first_factor, length_total // first_factor)


def combine_spectra(spec_real, spec_imag, width):
    filt_re = spec_real[..., :width]
    inner_re = spec_real[..., width : 2 * width]
    up_re = spec_real[..., 2 * width :]
    filt_im = spec_imag[..., :width]
    inner_im = spec_imag[..., width : 2 * width]
    up_im = spec_imag[..., 2 * width :]
    joined_real = jnp.concatenate(
        [
            filt_re * inner_re - filt_im * inner_im,
            filt_re * up_re + filt_im * up_im,
            up_re * inner_re + up_im * inner_im,
        ],
        axis=-1,
    )
    joined_imag = jnp.concatenate(
        [
            filt_re * inner_im + filt_im * inner_re,
            filt_re * up_im - filt_im * up_re,
            up_im * inner_re - up_re * inner_im,
        ],
        axis=-1,
    )
    return (joined_real, joined_imag)


def local_convolve(signals):
    length, branch_count, narrow = signals.shape
    total = 2 * length
    first_factor, second_factor = factors(total)
    flat = signals.reshape(length, branch_count * narrow)
    padded = jnp.concatenate([flat, jnp.zeros_like(flat)], axis=0).reshape(
        first_factor, second_factor, branch_count * narrow
    )
    first_index = jnp.arange(first_factor, dtype=jnp.int32)
    second_index = jnp.arange(second_factor, dtype=jnp.int32)
    cosine, sine_part = angles(first_index[:, None] * first_index[None, :], first_factor, -1.0)
    real_part = jnp.einsum("kn,nbm->kbm", cosine, padded, precision=precise_mode)
    imag_part = jnp.einsum("kn,nbm->kbm", sine_part, padded, precision=precise_mode)
    cosine, sine_part = angles(first_index[:, None] * second_index[None, :], total, -1.0)
    real_part, imag_part = rotate(real_part, imag_part, cosine[:, :, None], sine_part[:, :, None])
    real_part, imag_part = complex_einsum(
        "lb,kbm->klm",
        angles(second_index[:, None] * second_index[None, :], second_factor, -1.0),
        (real_part, imag_part),
    )
    real_part, imag_part = combine_spectra(real_part, imag_part, narrow)
    real_part, imag_part = complex_einsum(
        "bl,klm->kbm",
        angles(second_index[:, None] * second_index[None, :], second_factor, 1.0),
        (real_part, imag_part),
    )
    cosine, sine_part = angles(first_index[:, None] * second_index[None, :], total, 1.0)
    real_part, imag_part = rotate(real_part, imag_part, cosine[:, :, None], sine_part[:, :, None])
    cosine, sine_part = angles(first_index[:, None] * first_index[None, :], first_factor, 1.0)
    result = jnp.einsum("nk,kbm->nbm", cosine, real_part, precision=precise_mode) - jnp.einsum(
        "nk,kbm->nbm", sine_part, imag_part, precision=precise_mode
    )
    result = result.reshape(total, branch_count * narrow)[:length] / total
    return result.reshape(length, branch_count, narrow)


def shards(token_ids, embedding, proj_weight, filters, cotangent):
    tok_count = token_ids.shape[0]
    devices = lax.axis_size("seq")
    width = filters.shape[1]
    vocabulary = embedding.shape[0]
    width_rows, branches, red_count, piece = proj_weight.shape
    scale_factor = float(tok_count * devices) ** (-0.5)
    table = jnp.dot(
        embedding,
        proj_weight.reshape(width_rows, branches * red_count * piece),
        preferred_element_type=jnp.float32,
    )
    table = table.reshape(vocabulary, branches, red_count, piece)
    own_table = lax.psum_scatter(table, "red", scatter_dimension=2, tiled=True)
    full_table = lax.all_gather(own_table, "seq", axis=3, tiled=True)
    projected = jnp.take(full_table, token_ids, axis=0)
    projected = projected.reshape(tok_count, branches, width)
    queries = projected[:, 0]
    key_rows = projected[:, 1]
    value_rows = projected[:, 2]
    inner = key_rows * value_rows
    upstream = cotangent * queries
    stacked = jnp.stack([filters, inner, upstream], axis=1)
    whole_length = lax.all_to_all(stacked, "seq", split_axis=2, concat_axis=0, tiled=True)
    results = local_convolve(whole_length)
    returned = lax.all_to_all(results, "seq", split_axis=0, concat_axis=2, tiled=True)
    conv = returned[:, 0]
    grad_inner = returned[:, 1]
    filter_raw = returned[:, 2]
    output = queries * conv
    filter_grad = filter_raw * scale_factor
    branch_grads = jnp.stack(
        [cotangent * conv, grad_inner * value_rows, grad_inner * key_rows], axis=1
    ).astype(jnp.bfloat16)
    one_hot = (token_ids[:, None] == lax.iota(jnp.int32, vocabulary)[None, :]).astype(jnp.bfloat16)
    token_sums = lax.dot_general(
        one_hot,
        branch_grads.reshape(tok_count, branches * width),
        (((0,), (0,)), ((), ())),
        preferred_element_type=jnp.float32,
    )
    summed = lax.psum_scatter(
        token_sums.reshape(vocabulary, branches, width), "seq", scatter_dimension=2, tiled=True
    )
    gathered = lax.all_gather(summed[:, :, None, :], "red", axis=2, tiled=True)
    weight_grad = (
        lax.dot_general(
            embedding.astype(jnp.float32),
            gathered.reshape(vocabulary, branches * red_count * piece),
            (((0,), (0,)), ((), ())),
            precision=precise_mode,
        )
        * scale_factor
    )
    return (
        output,
        filter_grad,
        branch_grads,
        weight_grad.reshape(width_rows, branches, red_count, piece),
    )


def solution(mesh):
    in_specs = (
        P("seq"),
        P(None, "red"),
        P("red", None, None, "seq"),
        P("seq", "red"),
        P("seq", "red"),
    )
    out_specs = (
        P("seq", "red"),
        P("seq", "red"),
        P("seq", None, "red"),
        P("red", None, None, "seq"),
    )
    return jax.shard_map(shards, mesh=mesh, in_specs=in_specs, out_specs=out_specs, check_vma=False)
```

profile of v0, /device:TPU:0, one launch (start us, length us, event | category | flops | bytes accessed | tf_op | source)
XLA Modules:
  0.0 222.9 jit_solution(11435874289733762096)
XLA Ops:
  7.2 1.2 copy-done
  8.4 2.6 %fusion.2 = f32[512,3,4,32]{0,3,2,1:T(8,128)} fusion(bf16[512,1024]{1,0:T(8,128)(2,1)S(1)} %copy-done, bf16[1024,3,4,32]{0,3,2,1:T(8,128)(2,1)} %param.7), kind=kOutput, calls=%fused_computation.10 | convolution fusion | flops 402653184 | bytes 2621440 | tf_op jit(solution)/shard_map/dot_general | solution.py:109
  11.1 0.6 dynamic-slice
  11.7 46.1 %all-reduce.4.cloned.1.call-done = f32[512,3,4,32]{0,3,2,1:T(8,128)} async-done(((f32[512,3,4,32]{0,3,2,1:T(8,128)}), f32[512,3,4,32]{0,3,2,1:T(8,128)}) %all-reduce.4.cloned.1.call-update) | async-done | bytes 786448
  57.8 1.6 constant_dynamic-slice_fusion
  59.4 0.9 copy.120
  60.3 0.1 stack.18
  60.4 24.8 %all-gather.3.cloned.1.call-done = f32[512,3,1,256]{0,2,1,3:T(1,128)} async-done(((f32[512,3,1,32]{0,2,1,3:T(1,128)}), f32[512,3,1,256]{0,2,1,3:T(1,128)}) %all-gather.3.cloned.1.call-update) | async-done | bytes 1572880 | tf_op jit(solution)/shard_map/all_gather | solution.py:116
  85.2 4.7 %copy.121 = f32[512,3,1,256]{3,1,0,2:T(4,128)S(1)} copy(f32[512,3,1,256]{0,2,1,3:T(1,128)} %all-gather.3.cloned.1.call-done) | data formatting | bytes 3145728 | tf_op jit(solution)/shard_map/all_gather | solution.py:116
  89.9 1.6 gather_fusion
  91.5 1.2 broadcast_select_fusion
  92.8 0.8 copy-done.1
  93.6 0.2 slice_multiply_fusion.2
  93.9 0.1 stack.19
  94.0 0.5 copy-done.2
  94.5 0.3 pad_maximum_fusion.2
  94.8 1.0 copy.123
  95.9 3.5 %all-to-all-start = ((f32[128,3,256]{0,1,2:T(4,128)}), f32[128,3,256]{0,1,2:T(4,128)S(1)}, u32[]{:S(2)}, u32[]{:S(2)}) async-start(f32[128,3,256]{0,1,2:T(4,128)} %copy.123), calls=%async_computation | async-start | bytes 1048576 | tf_op jit(solution)/shard_map/all_to_all | solution.py:125
  99.4 0.2 reduce-scatter.5.cloned.1.call-start
  99.6 0.1 multiply_cosine_fusion.7
  99.7 0.1 copy.128
  99.8 0.1 multiply_sine_fusion.7
  99.9 0.1 copy.130
  99.9 0.1 multiply_sine_fusion.6
  100.0 9.0 %all-to-all-done = f32[128,3,256]{0,1,2:T(4,128)S(1)} async-done(((f32[128,3,256]{0,1,2:T(4,128)}), f32[128,3,256]{0,1,2:T(4,128)S(1)}, u32[]{:S(2)}, u32[]{:S(2)}) %all-to-all-start) | async-done | bytes 393248 | tf_op jit(solution)/shard_map/all_to_all | solution.py:125
  109.1 0.2 copy.125
  109.3 0.1 copy.183
  109.4 0.2 copy.157
  109.7 1.6 fusion.16
  111.3 1.9 multiply_subtract_fusion.3
  113.2 1.7 fusion.12
  115.0 1.7 fusion.8
  116.7 1.8 fusion.1
  118.5 1.8 fusion
  120.4 1.4 multiply_subtract_fusion.2
  121.7 1.1 multiply_add_fusion.2
  122.9 1.6 fusion.34
  124.5 1.6 fusion.32
  126.1 1.6 convolution_add_fusion
  127.7 2.0 subtract_bitcast_fusion
  129.6 1.6 fusion.4
  131.2 1.6 fusion.6
  132.8 0.1 fusion.19
  133.0 1.0 copy.148
  133.9 2.3 %reshape.135 = f32[1024,3,32]{2,1,0:T(4,128)S(1)} reshape(f32[16,64,96]{2,1,0:T(8,128)} %copy.148) | data formatting | bytes 786432 | tf_op jit(solution)/shard_map/div | solution.py:98
  136.2 1.3 reshape.139
  137.5 10.7 %all_to_all.33 = f32[8,1,12288]{2,1,0:T(1,128)S(1)} all-to-all(f32[8,1,12288]{2,1,0:T(1,128)S(1)} %reshape.139), channel_id=1, replica_groups=mesh['seq'=8,'red'=4] {'seq'}, dimensions={0} | all-to-all | bytes 786432 | tf_op jit(solution)/shard_map/all_to_all | solution.py:127
  148.3 0.5 broadcast.198
  148.8 1.6 reduce
  150.3 1.3 reshape.140
  151.7 0.6 copy.150
  152.4 0.1 copy.156
  152.5 1.5 slice_multiply_fusion.1
  154.0 0.1 copy.155
  154.2 0.1 copy.143
  154.3 0.5 maximum_convert_fusion
  154.7 0.2 copy.144
  154.9 1.6 fusion.21
  156.6 0.7 copy.146
  157.3 0.8 copy.145
  158.0 0.7 bitcast_multiply_fusion.1
  158.7 35.4 %reduce-scatter.5.cloned.1.call-done = f32[512,3,32]{0,2,1:T(8,128)} async-done(((f32[512,3,256]{0,2,1:T(8,128)}), f32[512,3,32]{0,2,1:T(8,128)}) %reduce-scatter.5.cloned.1.call-update) | async-done | bytes 196624 | tf_op jit(solution)/shard_map/reduce_scatter | solution.py:143
  194.1 19.7 %all-gather = f32[512,3,128]{0,2,1:T(8,128)S(1)} all-gather(f32[512,3,32]{0,2,1:T(8,128)} %reduce-scatter.5.cloned.1.call-done), channel_id=2, replica_groups=mesh['seq'=8,'red'=4] {'red'}, dimensions={2}, use_global_device_ids=true | all-gather | bytes 983040 | tf_op jit(solution)/shard_map/all_gather | solution.py:146
  213.9 2.5 %convolution_multiply_fusion = f32[384,1024]{1,0:T(8,128)} fusion(f32[512,384]{0,1:T(8,128)S(1)} %bitcast.117, bf16[512,1024]{1,0:T(8,128)(2,1)S(1)} %copy-done), kind=kOutput, calls=%fused_computation.1 | convolution fusion | flops 2416312320 | bytes 3407872 | tf_op jit(solution)/shard_map/dot_general | solution.py:148
  (28 shorter events, 0.4 us)
Async XLA Ops:
  7.2 1.2 copy-start
  7.2 3.9 %copy-start.8 = (u32[32]{0:T(128)S(1)}, u32[32]{0:T(128)}, u32[]{:S(2)}) copy-start(u32[32]{0:T(128)} %constant.91) | copy-start | bytes 388
  7.2 50.6 %all-reduce.4.cloned.1.call-start = ((), (), s32[]{:S(2)}) async-start(), calls=%async_computation.5 | async-start | bytes 1572864
  11.0 49.2 %copy-start.6 = (f32[128,256]{1,0:T(8,128)S(1)}, f32[128,256]{1,0:T(8,128)}, u32[]{:S(2)}) copy-start(f32[128,256]{1,0:T(8,128)} %param.8) | copy-start | bytes 393220
  11.0 49.4 %copy-start.7 = (s32[128]{0:T(128)S(1)}, s32[128]{0:T(128)}, u32[]{:S(2)}) copy-start(s32[128]{0:T(128)} %param.5) | copy-start | bytes 1540
  11.0 74.2 %all-gather.3.cloned.1.call-start = ((), (), s32[]{:S(2)}) async-start(), calls=%async_computation.3 | async-start | bytes 1769472 | tf_op jit(solution)/shard_map/all_gather | solution.py:116
  89.9 4.0 %copy-start.4 = (f32[128,256]{1,0:T(8,128)S(1)}, f32[128,256]{1,0:T(8,128)}, u32[]{:S(2)}) copy-start(f32[128,256]{1,0:T(8,128)} %param.9) | copy-start | bytes 393220
  92.8 0.8 copy-start.1
  93.8 0.7 copy-start.2
  95.9 13.2 %all-to-all-start = ((f32[128,3,256]{0,1,2:T(4,128)}), f32[128,3,256]{0,1,2:T(4,128)S(1)}, u32[]{:S(2)}, u32[]{:S(2)}) async-start(f32[128,3,256]{0,1,2:T(4,128)} %copy.123), calls=%async_computation | async-start | bytes 1048576 | tf_op jit(solution)/shard_map/all_to_all | solution.py:125
  99.4 94.7 %reduce-scatter.5.cloned.1.call-start = ((), (), s32[]{:S(2)}) async-start(), calls=%async_computation.4 | async-start | bytes 1769472 | tf_op jit(solution)/shard_map/reduce_scatter | solution.py:143
  152.3 1.8 copy-start.5
  156.5 1.5 copy-start.3
Sparse Core Ops, SparseCore 0:
  11.2 46.5 all-reduce.3
  60.4 24.8 all-gather.2
  156.7 37.3 reduce-scatter.4
where the time goes:
time: 224 us; the launch traced here: 223 us
  waiting for transfers between devices  115 us (51%)
  blocking collectives  30.4 us (14%)
  matrix products  27.3 us (12%)
  local copies, waits for them, and re-layouts  22.8 us (10%)
  between operations  14.2 us (6%)
  other arithmetic  9.04 us (4%)
  starting transfers between devices  3.8 us (2%)
    unnamed x4, waiting for transfers between devices  46.1 us
    reduce_scatter x1, waiting for transfers between devices, shards(): lax.psum_scatter(token_sums.reshape(vocabulary, branches, width), 'seq',...  35.4 us
    all_gather x1, waiting for transfers between devices, shards(): full_table = lax.all_gather(own_table, 'seq', axis=3, tiled=True)  24.8 us
    all_gather x1, blocking collectives, shards(): gathered = lax.all_gather(summed[:, :, None, :], 'red', axis=2, tiled=True)  19.7 us
    all_to_all x1, blocking collectives, shards(): lax.all_to_all(results, 'seq', split_axis=0, concat_axis=2, tiled=True)  10.7 us
    unnamed x28, local copies, waits for them, and re-layouts  9.24 us
    all_to_all x1, waiting for transfers between devices, shards(): lax.all_to_all(stacked, 'seq', split_axis=2, concat_axis=0, tiled=True)  8.98 us
    all_gather x1, local copies, waits for them, and re-layouts, shards(): full_table = lax.all_gather(own_table, 'seq', axis=3, tiled=True)  4.65 us
  transfers between devices with their start and end apart: 4, of which 4 were waited for; matrix products, arithmetic and copies ran while one was open for 1% of the time, Pallas kernels for 0%

commit v1 on v0

--- a/solution.py
+++ b/solution.py
@@ -1,11 +1,471 @@
+import functools
 import math
 
 import jax
 import jax.numpy as jnp
+import numpy as np
 from jax import lax
+from jax.experimental import pallas as pl
+from jax.experimental.pallas import tpu as pltpu
 from jax.sharding import PartitionSpec as P
 
 precise_mode = lax.Precision.HIGHEST
+MESH = pl.DeviceIdType.MESH
+VMEM = pl.BlockSpec(memory_space=pltpu.VMEM)
+NN = (((1,), (0,)), ((), ()))
+NT = (((1,), (1,)), ((), ()))
+
+
+def split(value):
+    high = value.astype(jnp.bfloat16)
+    low = (value - high.astype(jnp.float32)).astype(jnp.bfloat16)
+    return high, low
+
+
+def dot(left, right, dims=NN):
+    return lax.dot_general(left, right, dims, preferred_element_type=jnp.float32)
+
+
+def dot_split(value, matrix, dims=NN):
+    high, low = split(value)
+    both = dot(jnp.concatenate([high, low], axis=0), matrix, dims)
+    rows = value.shape[0]
+    return both[:rows] + both[rows:]
+
+
+def dot_both(value, matrix_high, matrix_low, dims=NN):
+    high, _ = split(value)
+    return dot_split(value, matrix_high, dims) + dot(high, matrix_low, dims)
+
+
+def transform_tables(block, blocks):
+    total = 2 * blocks * block
+    place = np.arange(block)
+    half = block // 2
+    tables = np.zeros((blocks, 2 * block, 2 * block))
+    even = 2 * np.pi * ((2 * blocks * place[:, None] * np.arange(half)[None, :]) % total) / total
+    odd = 2 * np.pi * ((place[:, None] * (blocks + 2 * blocks * np.arange(half))[None, :]) % total) / total
+    tables[0, :block, :half] = np.cos(even)
+    tables[0, :block, block : block + half] = np.sin(even)
+    tables[0, :block, block] = 1.0 - 2.0 * (place % 2)
+    tables[0, block:, half:block] = np.cos(odd)
+    tables[0, block:, block + half :] = np.sin(odd)
+    for residue in range(1, blocks):
+        freq = residue + 2 * blocks * np.arange(block)
+        psi = 2 * np.pi * ((place[:, None] * freq[None, :]) % total) / total
+        tables[residue, :block, :block] = np.cos(psi)
+        tables[residue, :block, block:] = np.sin(psi)
+        tables[residue, block:, :block] = -np.sin(psi)
+        tables[residue, block:, block:] = np.cos(psi)
+    tables = tables.astype(np.float32)
+    high = tables.astype(jnp.bfloat16)
+    low = (tables - high.astype(np.float32)).astype(jnp.bfloat16)
+    return high, low
+
+
+def phases(residue, blocks):
+    if residue == 0:
+        return [1.0] * blocks, [(-1.0) ** index for index in range(blocks)]
+    turn = [math.pi * ((residue * index) % (2 * blocks)) / blocks for index in range(blocks)]
+    return [math.cos(a) for a in turn], [math.sin(a) for a in turn]
+
+
+def weighted(terms, weights):
+    total = None
+    for term, weight in zip(terms, weights):
+        if abs(weight) < 1e-12:
+            continue
+        part = term if weight == 1.0 else term * weight
+        total = part if total is None else total + part
+    return total
+
+
+def greet(devices, count):
+    me = lax.axis_index("seq")
+    spot = lax.axis_index("red")
+    barrier = pltpu.get_barrier_semaphore()
+    for step in range(1, devices):
+        peer = lax.rem(me + step, devices)
+        pl.semaphore_signal(barrier, inc=1, device_id={"seq": peer}, device_id_type=MESH)
+
+    @pl.when(spot > 0)
+    def _():
+        pl.semaphore_signal(barrier, inc=1, device_id={"red": spot - 1}, device_id_type=MESH)
+
+    @pl.when(spot < count - 1)
+    def _():
+        pl.semaphore_signal(barrier, inc=1, device_id={"red": spot + 1}, device_id_type=MESH)
+
+    neighbours = jnp.where(spot > 0, 1, 0) + jnp.where(spot < count - 1, 1, 0)
+    pl.semaphore_wait(barrier, devices - 1 + neighbours)
+
+
+def exchange(devices, source, target, send_sem, recv_sem):
+    me = lax.axis_index("seq")
+    copies = []
+    for step in range(1, devices):
+        peer = lax.rem(me + step, devices)
+        copy = pltpu.make_async_remote_copy(
+            src_ref=source.at[peer],
+            dst_ref=target.at[me],
+            send_sem=send_sem.at[step - 1],
+            recv_sem=recv_sem.at[step - 1],
+            device_id={"seq": peer},
+            device_id_type=MESH,
+        )
+        copy.start()
+        copies.append(copy)
+    return copies
+
+
+def gather_kernel(
+    devices, count, tok_ref, emb_ref, wt_ref, filt_ref, cot_ref,
+    own_ref, sig_ref,
+    part, from_left, from_right, out_sig,
+    send_sig, recv_sig, send_right, recv_right, send_left, recv_left,
+):
+    me = lax.axis_index("seq")
+    spot = lax.axis_index("red")
+    branches, _, piece, _ = wt_ref.shape
+    tok_count, width = filt_ref.shape
+    filt_t = filt_ref[...].T
+    cot_t = cot_ref[...].T
+    tok_rows = jnp.broadcast_to(tok_ref[...].astype(jnp.float32), (8, tok_count))
+    for peer in range(devices):
+        out_sig[peer, :piece] = filt_t[peer * piece : (peer + 1) * piece]
+        out_sig[peer, piece : 2 * piece] = cot_t[peer * piece : (peer + 1) * piece]
+        out_sig[peer, 2 * piece :] = tok_rows
+    greet(devices, count)
+    copies = exchange(devices, out_sig, sig_ref, send_sig, recv_sig)
+    table = emb_ref[...]
+    for group in range(count):
+        rows = jnp.concatenate([wt_ref[branch, group] for branch in range(branches)], axis=0)
+        part[group] = dot(rows, table, NT)
+    sig_ref[me] = out_sig[me]
+
+    def hop(slot, target, sends, recvs, neighbour):
+        return pltpu.make_async_remote_copy(
+            src_ref=part.at[slot],
+            dst_ref=target.at[slot],
+            send_sem=sends.at[slot],
+            recv_sem=recvs.at[slot],
+            device_id={"red": neighbour},
+            device_id_type=MESH,
+        )
+
+    right = functools.partial(
+        hop, target=from_left, sends=send_right, recvs=recv_right,
+        neighbour=jnp.minimum(spot + 1, count - 1),
+    )
+    left = functools.partial(
+        hop, target=from_right, sends=send_left, recvs=recv_left,
+        neighbour=jnp.maximum(spot - 1, 0),
+    )
+    for step in range(count - 1):
+        goal = count - 1 - step
+
+        @pl.when(spot < goal)
+        def _():
+            @pl.when(spot > 0)
+            def _():
+                right(goal).wait_recv()
+                part[goal] = part[goal] + from_left[goal]
+
+            right(goal).start()
+
+        other = step
+
+        @pl.when(spot > other)
+        def _():
+            @pl.when(spot < count - 1)
+            def _():
+                left(other).wait_recv()
+                part[other] = part[other] + from_right[other]
+
+            left(other).start()
+
+    for goal in range(count):
+        @pl.when(spot == goal)
+        def _():
+            total = part[goal]
+            if goal > 0:
+                right(goal).wait_recv()
+                total = total + from_left[goal]
+            if goal < count - 1:
+                left(goal).wait_recv()
+                total = total + from_right[goal]
+            own_ref[...] = total
+
+        @pl.when(spot < goal)
+        def _():
+            right(goal).wait_send()
+
+        @pl.when(spot > goal)
+        def _():
+            left(goal).wait_send()
+
+    for copy in copies:
+        copy.wait()
+
+
+def convolve(signals, high_ref, low_ref, piece):
+    blocks, double, _ = high_ref.shape
+    block = double // 2
+    pieces = [signals[:, index * block : (index + 1) * block] for index in range(blocks)]
+    results = [None] * blocks
+    scale = 1.0 / (blocks * block)
+    for residue in range(blocks):
+        cosines, sines = phases(residue, blocks)
+        packed = jnp.concatenate([weighted(pieces, cosines), weighted(pieces, sines)], axis=1)
+        spectrum = dot_both(packed, high_ref[residue], low_ref[residue])
+        cos_part = spectrum[:, :block]
+        sin_part = spectrum[:, block:]
+        fc, ic, uc = (cos_part[at * piece : (at + 1) * piece] for at in range(3))
+        fs, i_s, us = (sin_part[at * piece : (at + 1) * piece] for at in range(3))
+        cc = [fc * ic, fc * uc, uc * ic]
+        ss = [fs * i_s, fs * us, us * i_s]
+        signs = [-1.0, 1.0, 1.0]
+        new_cos = [c + sign * s for c, s, sign in zip(cc, ss, signs)]
+        new_sin = [fc * i_s + fs * ic, fc * us - fs * uc, us * ic - uc * i_s]
+        new_cos = jnp.concatenate(new_cos, axis=0)
+        new_sin = jnp.concatenate(new_sin, axis=0)
+        if residue == 0:
+            first = lax.broadcasted_iota(jnp.int32, new_cos.shape, 1) == 0
+            new_cos = jnp.where(first, 0.5 * jnp.concatenate(cc, axis=0), new_cos)
+            new_sin = jnp.where(first, 0.5 * jnp.concatenate(ss, axis=0), new_sin)
+        joined = jnp.concatenate([new_cos, new_sin], axis=1) * scale
+        back = dot_both(joined, high_ref[residue], low_ref[residue], NT)
+        first_half = back[:, :block]
+        second_half = back[:, block:]
+        for index in range(blocks):
+            term = weighted([first_half, second_half], [cosines[index], sines[index]])
+            results[index] = term if results[index] is None else results[index] + term
+    return results
+
+
+def middle_kernel(scale_factor, own_ref, sig_ref, high_ref, low_ref, send_ref, sums_ref):
+    vocabulary = own_ref.shape[1]
+    devices, _, block = sig_ref.shape
+    piece = own_ref.shape[0] // 3
+    ids = jnp.concatenate([sig_ref[at, 2 * piece : 2 * piece + 1] for at in range(devices)], axis=1)
+    length = devices * block
+    rows = lax.broadcasted_iota(jnp.int32, (vocabulary, length), 0)
+    one_hot = jnp.where(rows == ids.astype(jnp.int32), 1.0, 0.0).astype(jnp.bfloat16)
+    projected = dot_split(own_ref[...], one_hot)
+    queries = projected[:piece]
+    key_rows = projected[piece : 2 * piece]
+    value_rows = projected[2 * piece :]
+    filters = jnp.concatenate([sig_ref[at, :piece] for at in range(devices)], axis=1)
+    cotangent = jnp.concatenate([sig_ref[at, piece : 2 * piece] for at in range(devices)], axis=1)
+    signals = jnp.concatenate([filters, key_rows * value_rows, cotangent * queries], axis=0)
+    results = convolve(signals, high_ref, low_ref, piece)
+    rounded = []
+    for at in range(devices):
+        lanes = slice(at * block, (at + 1) * block)
+        conv = results[at][:piece]
+        grad_inner = results[at][piece : 2 * piece]
+        grads = jnp.concatenate(
+            [
+                cotangent[:, lanes] * conv,
+                grad_inner * value_rows[:, lanes],
+                grad_inner * key_rows[:, lanes],
+            ],
+            axis=0,
+        ).astype(jnp.bfloat16)
+        rounded.append(grads)
+        send_ref[at, :piece] = queries[:, lanes] * conv
+        send_ref[at, piece : 2 * piece] = results[at][2 * piece :] * scale_factor
+        send_ref[at, 2 * piece :] = grads.astype(jnp.float32)
+    sums_ref[...] = dot(jnp.concatenate(rounded, axis=1), one_hot, NT)
+
+
+def return_kernel(
+    devices, count, send_ref, sums_ref, recv_ref, all_ref,
+    send_sem, recv_sem, send_right, recv_right, send_left, recv_left,
+):
+    me = lax.axis_index("seq")
+    spot = lax.axis_index("red")
+    greet(devices, count)
+
+    def hop(source, slot, sends, recvs, neighbour):
+        return pltpu.make_async_remote_copy(
+            src_ref=source,
+            dst_ref=all_ref.at[slot],
+            send_sem=sends.at[slot],
+            recv_sem=recvs.at[slot],
+            device_id={"red": neighbour},
+            device_id_type=MESH,
+        )
+
+    def right(source, slot):
+        return hop(source, slot, send_right, recv_right, jnp.minimum(spot + 1, count - 1))
+
+    def left(source, slot):
+        return hop(source, slot, send_left, recv_left, jnp.maximum(spot - 1, 0))
+
+    @pl.when(spot < count - 1)
+    def _():
+        right(sums_ref, spot).start()
+
+    @pl.when(spot > 0)
+    def _():
+        left(sums_ref, spot).start()
+
+    copies = exchange(devices, send_ref, recv_ref, send_sem, recv_sem)
+    all_ref[spot] = sums_ref[...]
+    recv_ref[me] = send_ref[me]
+    for step in range(1, count):
+        below = spot - step
+
+        @pl.when(below >= 0)
+        def _():
+            right(all_ref.at[below], below).wait_recv()
+
+            @pl.when(spot < count - 1)
+            def _():
+                right(all_ref.at[below], below).start()
+
+        above = spot + step
+
+        @pl.when(above < count)
+        def _():
+            left(all_ref.at[above], above).wait_recv()
+
+            @pl.when(spot > 0)
+            def _():
+                left(all_ref.at[above], above).start()
+
+    for step in range(count):
+        @pl.when((spot - step >= 0) & (spot < count - 1))
+        def _():
+            right(sums_ref, spot - step).wait_send()
+
+        @pl.when((spot + step < count) & (spot > 0))
+        def _():
+            left(sums_ref, spot + step).wait_send()
+
+    for copy in copies:
+        copy.wait()
+
+
+def final_kernel(scale_factor, emb_ref, recv_ref, all_ref, out_ref, filt_ref, grads_ref, weight_ref):
+    devices, rows, _ = recv_ref.shape
+    piece = rows // 5
+    count = all_ref.shape[0]
+    table = emb_ref[...]
+    for group in range(count):
+        product = dot_split(all_ref[group], table) * scale_factor
+        for branch in range(3):
+            weight_ref[branch, group] = product[branch * piece : (branch + 1) * piece]
+
+    def positions(at):
+        parts = [recv_ref[peer, at * piece : (at + 1) * piece] for peer in range(devices)]
+        return jnp.concatenate(parts, axis=0).T
+
+    out_ref[...] = positions(0)
+    filt_ref[...] = positions(1)
+    for branch in range(3):
+        grads_ref[branch] = positions(2 + branch).astype(jnp.bfloat16)
+
+
+def kernel_shards(devices, count, token_ids, embedding, proj_weight, filters, cotangent):
+    tok_count, width = filters.shape
+    vocabulary, depth = embedding.shape
+    _, branches, _, piece = proj_weight.shape
+    scale_factor = float(tok_count * devices) ** (-0.5)
+    rows = branches * piece
+    f32 = jnp.float32
+    dma = pltpu.SemaphoreType.DMA
+    weight_t = jnp.transpose(proj_weight, (1, 2, 3, 0))
+    own, signals = pl.pallas_call(
+        functools.partial(gather_kernel, devices, count),
+        out_shape=(
+            jax.ShapeDtypeStruct((rows, vocabulary), f32),
+            jax.ShapeDtypeStruct((devices, 2 * piece + 8, tok_count), f32),
+        ),
+        in_specs=[VMEM] * 5,
+        out_specs=(VMEM, VMEM),
+        scratch_shapes=[
+            pltpu.VMEM((count, rows, vocabulary), f32),
+            pltpu.VMEM((count, rows, vocabulary), f32),
+            pltpu.VMEM((count, rows, vocabulary), f32),
+            pltpu.VMEM((devices, 2 * piece + 8, tok_count), f32),
+            dma((devices - 1,)),
+            dma((devices - 1,)),
+            dma((count,)),
+            dma((count,)),
+            dma((count,)),
+            dma((count,)),
+        ],
+        compiler_params=pltpu.CompilerParams(collective_id=0, has_side_effects=True),
+        name="gather_signals",
+    )(token_ids.reshape(1, tok_count), embedding, weight_t, filters, cotangent)
+    high, low = transform_tables(tok_count, devices)
+    sending, sums = pl.pallas_call(
+        functools.partial(middle_kernel, scale_factor),
+        out_shape=(
+            jax.ShapeDtypeStruct((devices, 5 * piece, tok_count), f32),
+            jax.ShapeDtypeStruct((rows, vocabulary), f32),
+        ),
+        in_specs=[VMEM] * 4,
+        out_specs=(VMEM, VMEM),
+        name="convolve_channels",
+    )(own, signals, jnp.asarray(high), jnp.asarray(low))
+    received, all_sums = pl.pallas_call(
+        functools.partial(return_kernel, devices, count),
+        out_shape=(
+            jax.ShapeDtypeStruct((devices, 5 * piece, tok_count), f32),
+            jax.ShapeDtypeStruct((count, rows, vocabulary), f32),
+        ),
+        in_specs=[VMEM] * 2,
+        out_specs=(VMEM, VMEM),
+        scratch_shapes=[
+            dma((devices - 1,)),
+            dma((devices - 1,)),
+            dma((count,)),
+            dma((count,)),
+            dma((count,)),
+            dma((count,)),
+        ],
+        compiler_params=pltpu.CompilerParams(collective_id=1, has_side_effects=True),
+        name="return_results",
+    )(sending, sums)
+    output, filter_grad, grads, weight = pl.pallas_call(
+        functools.partial(final_kernel, scale_factor),
+        out_shape=(
+            jax.ShapeDtypeStruct((tok_count, width), f32),
+            jax.ShapeDtypeStruct((tok_count, width), f32),
+            jax.ShapeDtypeStruct((branches, tok_count, width), jnp.bfloat16),
+            jax.ShapeDtypeStruct((branches, count, piece, depth), f32),
+        ),
+        in_specs=[VMEM] * 3,
+        out_specs=(VMEM,) * 4,
+        name="finish",
+    )(embedding, received, all_sums)
+    return (
+        output,
+        filter_grad,
+        jnp.transpose(grads, (1, 0, 2)),
+        jnp.transpose(weight, (3, 0, 1, 2)),
+    )
+
+
+def fits_kernels(devices, count, token_ids, embedding, proj_weight, filters):
+    tok_count, width = filters.shape
+    vocabulary, depth = embedding.shape
+    _, branches, red_count, piece = proj_weight.shape
+    lanes = (tok_count, vocabulary, depth)
+    aligned = all(size % 128 == 0 for size in lanes) and piece % 16 == 0
+    tables = devices * (2 * tok_count) ** 2 * 4
+    one_hot = vocabulary * tok_count * devices * 8
+    held = 4 * branches * piece * vocabulary * (3 * count + 2)
+    return (
+        aligned
+        and branches == 3
+        and red_count == count
+        and width == devices * piece
+        and tables + one_hot + held < 40 * 2**20
+    )
 
 
 def angles(numbers, modulus, direction):
@@ -102,6 +562,11 @@
 def shards(token_ids, embedding, proj_weight, filters, cotangent):
     tok_count = token_ids.shape[0]
     devices = lax.axis_size("seq")
+    count = lax.axis_size("red")
+    if fits_kernels(devices, count, token_ids, embedding, proj_weight, filters):
+        return kernel_shards(
+            devices, count, token_ids, embedding, proj_weight, filters, cotangent
+        )
     width = filters.shape[1]
     vocabulary = embedding.shape[0]
     width_rows, branches, red_count, piece = proj_weight.shape

time: 224 us -> 59.9 us (0.27)
  waiting for transfers between devices: 115 us -> 0 us
  Pallas kernels: 0 us -> 59 us
  blocking collectives: 30.4 us -> 0 us
  matrix products: 27.3 us -> 0 us
  local copies, waits for them, and re-layouts: 22.8 us -> 0 us
  between operations: 14.2 us -> 0.65 us
  other arithmetic: 9.04 us -> 0 us
  starting transfers between devices: 3.8 us -> 0 us
    pallas_call x0 -> x4, Pallas kernels: none -> 59 us  [the longest x1 31.3 us: kernel_shards(): pl.pallas_call(functools.partial(gather_kernel, devices, count), out_shap...]
    unnamed x4 -> x0, waiting for transfers between devices: 46.1 us -> none
    reduce_scatter x1 -> x0, waiting for transfers between devices: 35.4 us -> none  [shards(): lax.psum_scatter(token_sums.reshape(vocabulary, branches, width), 'seq',...]
    dot_general x15 -> x0, matrix products: 27.3 us -> none  [the longest x2 3.76 us: complex_einsum(): jnp.einsum(formula, mat_imag, val_imag, precision=precise_mode)]
    all_gather x1 -> x0, waiting for transfers between devices: 24.8 us -> none  [shards(): full_table = lax.all_gather(own_table, 'seq', axis=3, tiled=True)]
    all_gather x1 -> x0, blocking collectives: 19.7 us -> none  [shards(): gathered = lax.all_gather(summed[:, :, None, :], 'red', axis=2, tiled=True)]
    all_to_all x1 -> x0, blocking collectives: 10.7 us -> none  [shards(): lax.all_to_all(results, 'seq', split_axis=0, concat_axis=2, tiled=True)]
    unnamed x28 -> x0, local copies, waits for them, and re-layouts: 9.24 us -> none
  transfers between devices with their start and end apart: 4 -> 0, of which waited for: 4 -> 0; matrix products, arithmetic and copies ran while one was open for 1% -> 0% of each run, Pallas kernels for 0% -> 0%
where the time goes in v1:
time: 59.9 us; the launch traced here: 59.6 us
  Pallas kernels  59 us (98%)
  between operations  0.65 us (1%)
    pallas_call x1, Pallas kernels, kernel_shards(): pl.pallas_call(functools.partial(gather_kernel, devices, count), out_shap...  31.3 us
    pallas_call x1, Pallas kernels, kernel_shards(): pl.pallas_call(functools.partial(return_kernel, devices, count), out_shap...  19.1 us
    pallas_call x1, Pallas kernels, kernel_shards(): pl.pallas_call(functools.partial(middle_kernel, scale_factor), out_shape=...  4.79 us
    pallas_call x1, Pallas kernels, kernel_shards(): pl.pallas_call(functools.partial(final_kernel, scale_factor), out_shape=(...  3.83 us

profile of v1, /device:TPU:0, one launch (start us, length us, event | category | flops | bytes accessed | tf_op | source)
XLA Modules:
  0.0 59.6 jit_solution(1405967621633860203)
XLA Ops:
  0.6 31.3 %gather_signals.1 = (f32[96,512]{1,0:T(8,128)}, f32[8,72,128]{2,1,0:T(8,128)}) custom-call(s32[1,128]{1,0:T(1,128)} %bitcast.5, bf16[512,1024]{1,0:T(8,128)(2,1)} %emb_ref.3, bf16[3,4,32,1024]{3,2,1,0:T(8,128)(2,1)} %bitcast.4, f32[128,256]{1,0:T(8,128)} %filt_ref.1, f32[128,256]{1,0:T(8,128)} %cot_ref.1), custom_call_target="tpu_custom_call" | custom-call | tf_op jit(solution)/shard_map/gather_signals/pallas_call | solution.py:380
  31.9 4.8 %convolve_channels.1 = (f32[8,160,128]{2,1,0:T(8,128)}, f32[96,512]{1,0:T(8,128)}) custom-call(f32[96,512]{1,0:T(8,128)} %get-tuple-element.14.own_ref, f32[8,72,128]{2,1,0:T(8,128)} %get-tuple-element.15.sig_ref, bf16[8,256,256]{2,1,0:T(8,128)(2,1)} %constant.4.clone.high_ref, bf16[8,256,256]{2,1,0:T(8,128)(2,1)} %constant.5.clone.low_ref), custom_call_target="tpu_custom_call" | custom-call | tf_op jit(solution)/shard_map/convolve_channels/pallas_call | solution.py:404
  36.7 19.1 %return_results.1 = (f32[8,160,128]{2,1,0:T(8,128)}, f32[4,96,512]{2,1,0:T(8,128)}) custom-call(f32[8,160,128]{2,1,0:T(8,128)} %get-tuple-element.16.send_ref, f32[96,512]{1,0:T(8,128)} %get-tuple-element.17.sums_ref), custom_call_target="tpu_custom_call" | custom-call | tf_op jit(solution)/shard_map/return_results/pallas_call | solution.py:414
  55.8 3.8 %finish.1 = (f32[128,256]{1,0:T(8,128)}, f32[128,256]{1,0:T(8,128)}, bf16[3,128,256]{2,1,0:T(8,128)(2,1)}, f32[3,4,32,1024]{3,2,1,0:T(8,128)}) custom-call(bf16[512,1024]{1,0:T(8,128)(2,1)} %emb_ref.3, f32[8,160,128]{2,1,0:T(8,128)} %get-tuple-element.18.recv_ref, f32[4,96,512]{2,1,0:T(8,128)} %get-tuple-element.19.all_ref), custom_call_target="tpu_custom_call" | custom-call | tf_op jit(solution)/shard_map/finish/pallas_call | solution.py:433

commit v2 on v1

--- a/solution.py
+++ b/solution.py
@@ -161,10 +161,10 @@
         hop, target=from_right, sends=send_left, recvs=recv_left,
         neighbour=jnp.maximum(spot - 1, 0),
     )
-    for step in range(count - 1):
-        goal = count - 1 - step
-
-        @pl.when(spot < goal)
+    for tick in range(2 * count - 2):
+        goal = count - 1 - (tick - spot)
+
+        @pl.when((tick >= spot) & (spot < goal))
         def _():
             @pl.when(spot > 0)
             def _():
@@ -173,9 +173,9 @@
 
             right(goal).start()
 
-        other = step
-
-        @pl.when(spot > other)
+        other = tick - (count - 1 - spot)
+
+        @pl.when((other >= 0) & (spot > other))
         def _():
             @pl.when(spot < count - 1)
             def _():

time: 59.9 us -> 55.4 us (0.925)
  Pallas kernels: 59 us -> 54.5 us
    pallas_call x1, Pallas kernels: 31.3 us -> 26.3 us  [kernel_shards(): pl.pallas_call(functools.partial(gather_kernel, devices, count), out_shap...]
where the time goes in v2:
time: 55.4 us; the launch traced here: 55.1 us
  Pallas kernels  54.5 us (98%)
  between operations  0.65 us (1%)
    pallas_call x1, Pallas kernels, kernel_shards(): pl.pallas_call(functools.partial(gather_kernel, devices, count), out_shap...  26.3 us
    pallas_call x1, Pallas kernels, kernel_shards(): pl.pallas_call(functools.partial(return_kernel, devices, count), out_shap...  19.6 us
    pallas_call x1, Pallas kernels, kernel_shards(): pl.pallas_call(functools.partial(middle_kernel, scale_factor), out_shape=...  4.78 us
    pallas_call x1, Pallas kernels, kernel_shards(): pl.pallas_call(functools.partial(final_kernel, scale_factor), out_shape=(...  3.83 us

profile of v2, /device:TPU:0, one launch (start us, length us, event | category | flops | bytes accessed | tf_op | source)
XLA Modules:
  0.0 55.1 jit_solution(4459461898466938563)
XLA Ops:
  0.6 26.3 %gather_signals.1 = (f32[96,512]{1,0:T(8,128)}, f32[8,72,128]{2,1,0:T(8,128)}) custom-call(s32[1,128]{1,0:T(1,128)} %bitcast.5, bf16[512,1024]{1,0:T(8,128)(2,1)} %emb_ref.3, bf16[3,4,32,1024]{3,2,1,0:T(8,128)(2,1)} %bitcast.4, f32[128,256]{1,0:T(8,128)} %filt_ref.1, f32[128,256]{1,0:T(8,128)} %cot_ref.1), custom_call_target="tpu_custom_call" | custom-call | tf_op jit(solution)/shard_map/gather_signals/pallas_call | solution.py:380
  27.0 4.8 %convolve_channels.1 = (f32[8,160,128]{2,1,0:T(8,128)}, f32[96,512]{1,0:T(8,128)}) custom-call(f32[96,512]{1,0:T(8,128)} %get-tuple-element.14.own_ref, f32[8,72,128]{2,1,0:T(8,128)} %get-tuple-element.15.sig_ref, bf16[8,256,256]{2,1,0:T(8,128)(2,1)} %constant.4.clone.high_ref, bf16[8,256,256]{2,1,0:T(8,128)(2,1)} %constant.5.clone.low_ref), custom_call_target="tpu_custom_call" | custom-call | tf_op jit(solution)/shard_map/convolve_channels/pallas_call | solution.py:404
  31.7 19.6 %return_results.1 = (f32[8,160,128]{2,1,0:T(8,128)}, f32[4,96,512]{2,1,0:T(8,128)}) custom-call(f32[8,160,128]{2,1,0:T(8,128)} %get-tuple-element.16.send_ref, f32[96,512]{1,0:T(8,128)} %get-tuple-element.17.sums_ref), custom_call_target="tpu_custom_call" | custom-call | tf_op jit(solution)/shard_map/return_results/pallas_call | solution.py:414
  51.3 3.8 %finish.1 = (f32[128,256]{1,0:T(8,128)}, f32[128,256]{1,0:T(8,128)}, bf16[3,128,256]{2,1,0:T(8,128)(2,1)}, f32[3,4,32,1024]{3,2,1,0:T(8,128)}) custom-call(bf16[512,1024]{1,0:T(8,128)(2,1)} %emb_ref.3, f32[8,160,128]{2,1,0:T(8,128)} %get-tuple-element.18.recv_ref, f32[4,96,512]{2,1,0:T(8,128)} %get-tuple-element.19.all_ref), custom_call_target="tpu_custom_call" | custom-call | tf_op jit(solution)/shard_map/finish/pallas_call | solution.py:433

commit v3 on v0

--- a/solution.py
+++ b/solution.py
@@ -1,11 +1,510 @@
+import functools
 import math
 
 import jax
 import jax.numpy as jnp
+import numpy as np
 from jax import lax
+from jax.experimental import pallas as pl
+from jax.experimental.pallas import tpu as pltpu
 from jax.sharding import PartitionSpec as P
 
 precise_mode = lax.Precision.HIGHEST
+MESH = pl.DeviceIdType.MESH
+VMEM = pl.BlockSpec(memory_space=pltpu.VMEM)
+CHUNKS = 2
+NN = (((1,), (0,)), ((), ()))
+NT = (((1,), (1,)), ((), ()))
+
+
+def split(value):
+    high = value.astype(jnp.bfloat16)
+    low = (value - high.astype(jnp.float32)).astype(jnp.bfloat16)
+    return high, low
+
+
+def dot(left, right, dims=NN):
+    return lax.dot_general(left, right, dims, preferred_element_type=jnp.float32)
+
+
+def dot_split(value, matrix, dims=NN):
+    high, low = split(value)
+    both = dot(jnp.concatenate([high, low], axis=0), matrix, dims)
+    rows = value.shape[0]
+    return both[:rows] + both[rows:]
+
+
+def dot_both(value, matrix_high, matrix_low, dims=NN):
+    high, _ = split(value)
+    return dot_split(value, matrix_high, dims) + dot(high, matrix_low, dims)
+
+
+def transform_tables(block, blocks):
+    total = 2 * blocks * block
+    place = np.arange(block)
+    half = block // 2
+    tables = np.zeros((blocks, 2 * block, 2 * block))
+    even = 2 * np.pi * ((2 * blocks * place[:, None] * np.arange(half)[None, :]) % total) / total
+    odd = 2 * np.pi * ((place[:, None] * (blocks + 2 * blocks * np.arange(half))[None, :]) % total) / total
+    tables[0, :block, :half] = np.cos(even)
+    tables[0, :block, block : block + half] = np.sin(even)
+    tables[0, :block, block] = 1.0 - 2.0 * (place % 2)
+    tables[0, block:, half:block] = np.cos(odd)
+    tables[0, block:, block + half :] = np.sin(odd)
+    for residue in range(1, blocks):
+        freq = residue + 2 * blocks * np.arange(block)
+        psi = 2 * np.pi * ((place[:, None] * freq[None, :]) % total) / total
+        tables[residue, :block, :block] = np.cos(psi)
+        tables[residue, :block, block:] = np.sin(psi)
+        tables[residue, block:, :block] = -np.sin(psi)
+        tables[residue, block:, block:] = np.cos(psi)
+    tables = tables.astype(np.float32)
+    high = tables.astype(jnp.bfloat16)
+    low = (tables - high.astype(np.float32)).astype(jnp.bfloat16)
+    return high, low
+
+
+def phases(residue, blocks):
+    if residue == 0:
+        return [1.0] * blocks, [(-1.0) ** index for index in range(blocks)]
+    turn = [math.pi * ((residue * index) % (2 * blocks)) / blocks for index in range(blocks)]
+    return [math.cos(a) for a in turn], [math.sin(a) for a in turn]
+
+
+def weighted(terms, weights):
+    total = None
+    for term, weight in zip(terms, weights):
+        if abs(weight) < 1e-12:
+            continue
+        part = term if weight == 1.0 else term * weight
+        total = part if total is None else total + part
+    return total
+
+
+def convolve(signals, high_ref, low_ref, piece, beside):
+    blocks, double, _ = high_ref.shape
+    block = double // 2
+    pieces = [signals[:, index * block : (index + 1) * block] for index in range(blocks)]
+    results = [None] * blocks
+    scale = 1.0 / (blocks * block)
+    for residue in range(blocks):
+        if residue == blocks // 2:
+            beside()
+        cosines, sines = phases(residue, blocks)
+        packed = jnp.concatenate([weighted(pieces, cosines), weighted(pieces, sines)], axis=1)
+        spectrum = dot_both(packed, high_ref[residue], low_ref[residue])
+        cos_part = spectrum[:, :block]
+        sin_part = spectrum[:, block:]
+        fc, ic, uc = (cos_part[at * piece : (at + 1) * piece] for at in range(3))
+        fs, i_s, us = (sin_part[at * piece : (at + 1) * piece] for at in range(3))
+        cc = [fc * ic, fc * uc, uc * ic]
+        ss = [fs * i_s, fs * us, us * i_s]
+        signs = [-1.0, 1.0, 1.0]
+        new_cos = [c + sign * s for c, s, sign in zip(cc, ss, signs)]
+        new_sin = [fc * i_s + fs * ic, fc * us - fs * uc, us * ic - uc * i_s]
+        new_cos = jnp.concatenate(new_cos, axis=0)
+        new_sin = jnp.concatenate(new_sin, axis=0)
+        if residue == 0:
+            first = lax.broadcasted_iota(jnp.int32, new_cos.shape, 1) == 0
+            new_cos = jnp.where(first, 0.5 * jnp.concatenate(cc, axis=0), new_cos)
+            new_sin = jnp.where(first, 0.5 * jnp.concatenate(ss, axis=0), new_sin)
+        joined = jnp.concatenate([new_cos, new_sin], axis=1) * scale
+        back = dot_both(joined, high_ref[residue], low_ref[residue], NT)
+        first_half = back[:, :block]
+        second_half = back[:, block:]
+        for index in range(blocks):
+            term = weighted([first_half, second_half], [cosines[index], sines[index]])
+            results[index] = term if results[index] is None else results[index] + term
+    return results
+
+
+def greet(devices, count):
+    me = lax.axis_index("seq")
+    spot = lax.axis_index("red")
+    barrier = pltpu.get_barrier_semaphore()
+    for step in range(1, devices):
+        peer = lax.rem(me + step, devices)
+        pl.semaphore_signal(barrier, inc=1, device_id={"seq": peer}, device_id_type=MESH)
+
+    @pl.when(spot > 0)
+    def _():
+        pl.semaphore_signal(barrier, inc=1, device_id={"red": spot - 1}, device_id_type=MESH)
+
+    @pl.when(spot < count - 1)
+    def _():
+        pl.semaphore_signal(barrier, inc=1, device_id={"red": spot + 1}, device_id_type=MESH)
+
+
+def meet(devices, count):
+    spot = lax.axis_index("red")
+    neighbours = jnp.where(spot > 0, 1, 0) + jnp.where(spot < count - 1, 1, 0)
+    pl.semaphore_wait(pltpu.get_barrier_semaphore(), devices - 1 + neighbours)
+
+
+def exchange(devices, source, target, send_sem, recv_sem, base):
+    me = lax.axis_index("seq")
+    copies = []
+    for step in range(1, devices):
+        peer = lax.rem(me + step, devices)
+        copy = pltpu.make_async_remote_copy(
+            src_ref=source(peer),
+            dst_ref=target(me),
+            send_sem=send_sem.at[base + step - 1],
+            recv_sem=recv_sem.at[base + step - 1],
+            device_id={"seq": peer},
+            device_id_type=MESH,
+        )
+        copy.start()
+        copies.append(copy)
+    return copies
+
+
+def main_kernel(
+    devices, count, chunks, scale_factor,
+    tok_ref, emb_ref, wt_ref, filt_ref, cot_ref, high_hbm, low_hbm,
+    recv_ref, all_ref,
+    part, from_left, from_right, out_sig, sig, sending, one_hot, high_ref, low_ref,
+    table_sem, sig_send, sig_recv, res_send, res_recv,
+    right_send, right_recv, left_send, left_recv,
+    up_send, up_recv, down_send, down_recv,
+):
+    me = lax.axis_index("seq")
+    spot = lax.axis_index("red")
+    branches, _, piece, _ = wt_ref.shape
+    tok_count, width = filt_ref.shape
+    vocabulary = emb_ref.shape[0]
+    sub = piece // chunks
+    greet(devices, count)
+    tables = [
+        pltpu.make_async_copy(high_hbm, high_ref, table_sem.at[0]),
+        pltpu.make_async_copy(low_hbm, low_ref, table_sem.at[1]),
+    ]
+    for copy in tables:
+        copy.start()
+    above_spot = jnp.minimum(spot + 1, count - 1)
+    below_spot = jnp.maximum(spot - 1, 0)
+
+    def hop(source, target, slot, sends, recvs, neighbour):
+        return pltpu.make_async_remote_copy(
+            src_ref=source.at[slot],
+            dst_ref=target.at[slot],
+            send_sem=sends.at[slot],
+            recv_sem=recvs.at[slot],
+            device_id={"red": neighbour},
+            device_id_type=MESH,
+        )
+
+    def right(slot):
+        return hop(part, from_left, slot, right_send, right_recv, above_spot)
+
+    def left(slot):
+        return hop(part, from_right, slot, left_send, left_recv, below_spot)
+
+    def up(slot):
+        return hop(all_ref, all_ref, slot, up_send, up_recv, above_spot)
+
+    def down(slot):
+        return hop(all_ref, all_ref, slot, down_send, down_recv, below_spot)
+
+    def products(chunk):
+        table = emb_ref[...]
+        for group in range(count):
+            rows = [wt_ref[b, group, chunk * sub : (chunk + 1) * sub] for b in range(branches)]
+            part[chunk * count + group] = dot(jnp.concatenate(rows, axis=0), table, NT)
+
+    def first_hops(chunk):
+        base = chunk * count
+
+        @pl.when(spot == 0)
+        def _():
+            for goal in range(count - 1, 0, -1):
+                right(base + goal).start()
+
+        @pl.when(spot == count - 1)
+        def _():
+            for goal in range(count - 1):
+                left(base + goal).start()
+
+    def middle_hops(chunk):
+        base = chunk * count
+        for tick in range(1, count - 1):
+            goal = count - 1 - (tick - spot)
+
+            @pl.when((spot > 0) & (tick >= spot) & (spot < goal))
+            def _():
+                right(base + goal).wait_recv()
+                part[base + goal] = part[base + goal] + from_left[base + goal]
+                right(base + goal).start()
+
+            other = tick - (count - 1 - spot)
+
+            @pl.when((spot < count - 1) & (other >= 0) & (spot > other))
+            def _():
+                left(base + other).wait_recv()
+                part[base + other] = part[base + other] + from_right[base + other]
+                left(base + other).start()
+
+    def arrive(chunk):
+        slot = chunk * count + spot
+
+        @pl.when(spot > 0)
+        def _():
+            right(slot).wait_recv()
+            part[slot] = part[slot] + from_left[slot]
+
+        @pl.when(spot < count - 1)
+        def _():
+            left(slot).wait_recv()
+            part[slot] = part[slot] + from_right[slot]
+
+        return part[slot]
+
+    def share(chunk):
+        slot = chunk * count + spot
+
+        @pl.when(spot < count - 1)
+        def _():
+            up(slot).start()
+
+        @pl.when(spot > 0)
+        def _():
+            down(slot).start()
+
+    def relay(chunk, step):
+        base = chunk * count
+        below = spot - step
+
+        @pl.when(below >= 0)
+        def _():
+            up(base + below).wait_recv()
+
+            @pl.when(spot < count - 1)
+            def _():
+                up(base + below).start()
+
+        above = spot + step
+
+        @pl.when(above < count)
+        def _():
+            down(base + above).wait_recv()
+
+            @pl.when(spot > 0)
+            def _():
+                down(base + above).start()
+
+    def signal_rows(start, rows):
+        return jnp.concatenate([sig[at, start : start + rows] for at in range(devices)], axis=1)
+
+    def channels(chunk, own, beside):
+        projected = dot_split(own, one_hot[...])
+        queries = projected[:sub]
+        key_rows = projected[sub : 2 * sub]
+        value_rows = projected[2 * sub :]
+        filters = signal_rows(chunk * sub, sub)
+        cotangent = signal_rows(piece + chunk * sub, sub)
+        signals = jnp.concatenate([filters, key_rows * value_rows, cotangent * queries], axis=0)
+        results = convolve(signals, high_ref, low_ref, sub, beside)
+        rounded = []
+        for at in range(devices):
+            lanes = slice(at * tok_count, (at + 1) * tok_count)
+            conv = results[at][:sub]
+            grad_inner = results[at][sub : 2 * sub]
+            grads = jnp.concatenate(
+                [
+                    cotangent[:, lanes] * conv,
+                    grad_inner * value_rows[:, lanes],
+                    grad_inner * key_rows[:, lanes],
+                ],
+                axis=0,
+            ).astype(jnp.bfloat16)
+            rounded.append(grads)
+            sending[chunk, at, :sub] = queries[:, lanes] * conv
+            sending[chunk, at, sub : 2 * sub] = results[at][2 * sub :] * scale_factor
+            sending[chunk, at, 2 * sub :] = grads.astype(jnp.float32)
+        all_ref[chunk * count + spot] = dot(jnp.concatenate(rounded, axis=1), one_hot[...], NT)
+
+    filt_t = filt_ref[...].T
+    cot_t = cot_ref[...].T
+    tok_rows = jnp.broadcast_to(tok_ref[...].astype(jnp.float32), (8, tok_count))
+    for peer in range(devices):
+        out_sig[peer, :piece] = filt_t[peer * piece : (peer + 1) * piece]
+        out_sig[peer, piece : 2 * piece] = cot_t[peer * piece : (peer + 1) * piece]
+        out_sig[peer, 2 * piece :] = tok_rows
+    products(0)
+    meet(devices, count)
+    first_hops(0)
+    copies = exchange(devices, out_sig.at.__getitem__, sig.at.__getitem__, sig_send, sig_recv, 0)
+    for chunk in range(1, chunks):
+        products(chunk)
+        first_hops(chunk)
+    sig[me] = out_sig[me]
+    for copy in copies:
+        copy.wait_recv()
+    ids = signal_rows(2 * piece, 1).astype(jnp.int32)
+    vocab_rows = lax.broadcasted_iota(jnp.int32, (vocabulary, devices * tok_count), 0)
+    one_hot[...] = jnp.where(vocab_rows == ids, 1.0, 0.0).astype(jnp.bfloat16)
+    sent = list(copies)
+    arrivals = []
+    for chunk in range(chunks):
+        middle_hops(chunk)
+        if chunk > 0:
+            relay(chunk - 1, 1)
+        own = arrive(chunk)
+        if chunk == 0:
+            for copy in tables:
+                copy.wait()
+
+        def beside(chunk=chunk):
+            if chunk > 0 and count > 2:
+                relay(chunk - 1, 2)
+
+        channels(chunk, own, beside)
+        share(chunk)
+        more = exchange(
+            devices,
+            lambda peer, chunk=chunk: sending.at[chunk, peer],
+            lambda slot, chunk=chunk: recv_ref.at[chunk, slot],
+            res_send, res_recv, chunk * (devices - 1),
+        )
+        recv_ref[chunk, me] = sending[chunk, me]
+        sent += more
+        arrivals += more
+        if chunk > 0:
+            for step in range(3, count):
+                relay(chunk - 1, step)
+    for step in range(1, count):
+        relay(chunks - 1, step)
+    for chunk in range(chunks):
+        base = chunk * count
+        for goal in range(count):
+            @pl.when(spot < goal)
+            def _():
+                right(base + goal).wait_send()
+
+            @pl.when(spot > goal)
+            def _():
+                left(base + goal).wait_send()
+
+        for step in range(count):
+            @pl.when((spot - step >= 0) & (spot < count - 1))
+            def _():
+                up(base + spot - step).wait_send()
+
+            @pl.when((spot + step < count) & (spot > 0))
+            def _():
+                down(base + spot + step).wait_send()
+
+    for copy in sent:
+        copy.wait_send()
+    for copy in arrivals:
+        copy.wait_recv()
+
+
+def final_kernel(scale_factor, emb_ref, recv_ref, all_ref, out_ref, filt_ref, grads_ref, weight_ref):
+    chunks, devices, rows, _ = recv_ref.shape
+    sub = rows // 5
+    count = all_ref.shape[0] // chunks
+    table = emb_ref[...]
+    for chunk in range(chunks):
+        for group in range(count):
+            product = dot_split(all_ref[chunk * count + group], table) * scale_factor
+            for branch in range(3):
+                weight_ref[branch, group, chunk * sub : (chunk + 1) * sub] = product[
+                    branch * sub : (branch + 1) * sub
+                ]
+
+    def positions(at):
+        parts = [
+            recv_ref[chunk, peer, at * sub : (at + 1) * sub]
+            for peer in range(devices)
+            for chunk in range(chunks)
+        ]
+        return jnp.concatenate(parts, axis=0).T
+
+    out_ref[...] = positions(0)
+    filt_ref[...] = positions(1)
+    for branch in range(3):
+        grads_ref[branch] = positions(2 + branch).astype(jnp.bfloat16)
+
+
+def kernel_shards(devices, count, token_ids, embedding, proj_weight, filters, cotangent):
+    tok_count, width = filters.shape
+    vocabulary, depth = embedding.shape
+    _, branches, _, piece = proj_weight.shape
+    scale_factor = float(tok_count * devices) ** (-0.5)
+    chunks = CHUNKS
+    rows = branches * piece // chunks
+    f32 = jnp.float32
+    dma = pltpu.SemaphoreType.DMA
+    weight_t = jnp.transpose(proj_weight, (1, 2, 3, 0))
+    high, low = transform_tables(tok_count, devices)
+    block = (chunks * count, rows, vocabulary)
+    message = (devices, 2 * piece + 8, tok_count)
+    answer = (chunks, devices, 5 * piece // chunks, tok_count)
+    received, all_sums = pl.pallas_call(
+        functools.partial(main_kernel, devices, count, chunks, scale_factor),
+        out_shape=(jax.ShapeDtypeStruct(answer, f32), jax.ShapeDtypeStruct(block, f32)),
+        in_specs=[VMEM] * 5 + [pl.BlockSpec(memory_space=pl.ANY)] * 2,
+        out_specs=(VMEM, VMEM),
+        scratch_shapes=[
+            pltpu.VMEM(block, f32),
+            pltpu.VMEM(block, f32),
+            pltpu.VMEM(block, f32),
+            pltpu.VMEM(message, f32),
+            pltpu.VMEM(message, f32),
+            pltpu.VMEM(answer, f32),
+            pltpu.VMEM((vocabulary, devices * tok_count), jnp.bfloat16),
+            pltpu.VMEM(high.shape, jnp.bfloat16),
+            pltpu.VMEM(low.shape, jnp.bfloat16),
+            dma((2,)),
+            dma((devices - 1,)),
+            dma((devices - 1,)),
+            dma((chunks * (devices - 1),)),
+            dma((chunks * (devices - 1),)),
+        ]
+        + [dma((chunks * count,))] * 8,
+        compiler_params=pltpu.CompilerParams(collective_id=0, has_side_effects=True),
+        name="hyena_exchange",
+    )(
+        token_ids.reshape(1, tok_count), embedding, weight_t, filters, cotangent,
+        jnp.asarray(high), jnp.asarray(low),
+    )
+    output, filter_grad, grads, weight = pl.pallas_call(
+        functools.partial(final_kernel, scale_factor),
+        out_shape=(
+            jax.ShapeDtypeStruct((tok_count, width), f32),
+            jax.ShapeDtypeStruct((tok_count, width), f32),
+            jax.ShapeDtypeStruct((branches, tok_count, width), jnp.bfloat16),
+            jax.ShapeDtypeStruct((branches, count, piece, depth), f32),
+        ),
+        in_specs=[VMEM] * 3,
+        out_specs=(VMEM,) * 4,
+        name="finish",
+    )(embedding, received, all_sums)
+    return (
+        output,
+        filter_grad,
+        jnp.transpose(grads, (1, 0, 2)),
+        jnp.transpose(weight, (3, 0, 1, 2)),
+    )
+
+
+def fits_kernels(devices, count, token_ids, embedding, proj_weight, filters):
+    tok_count, width = filters.shape
+    vocabulary, depth = embedding.shape
+    _, branches, red_count, piece = proj_weight.shape
+    lanes = (tok_count, vocabulary, depth)
+    aligned = all(size % 128 == 0 for size in lanes) and piece % (16 * CHUNKS) == 0
+    tables = devices * (2 * tok_count) ** 2 * 4
+    one_hot = vocabulary * tok_count * devices * 8
+    held = 4 * branches * piece * vocabulary * (3 * count + 2)
+    return (
+        aligned
+        and branches == 3
+        and red_count == count
+        and width == devices * piece
+        and tables + one_hot + held < 40 * 2**20
+    )
 
 
 def angles(numbers, modulus, direction):
@@ -102,6 +601,11 @@
 def shards(token_ids, embedding, proj_weight, filters, cotangent):
     tok_count = token_ids.shape[0]
     devices = lax.axis_size("seq")
+    count = lax.axis_size("red")
+    if fits_kernels(devices, count, token_ids, embedding, proj_weight, filters):
+        return kernel_shards(
+            devices, count, token_ids, embedding, proj_weight, filters, cotangent
+        )
     width = filters.shape[1]
     vocabulary = embedding.shape[0]
     width_rows, branches, red_count, piece = proj_weight.shape

time: 224 us -> 53 us (0.24)
  waiting for transfers between devices: 115 us -> 0 us
  Pallas kernels: 0 us -> 52.1 us
  blocking collectives: 30.4 us -> 0 us
  matrix products: 27.3 us -> 0 us
  local copies, waits for them, and re-layouts: 22.8 us -> 0 us
  between operations: 14.2 us -> 0.64 us
  other arithmetic: 9.04 us -> 0 us
  starting transfers between devices: 3.8 us -> 0 us
    pallas_call x0 -> x2, Pallas kernels: none -> 52.2 us  [the longest x1 47.9 us: kernel_shards(): pl.pallas_call(functools.partial(main_kernel, devices, count, chunks, sca...]
    unnamed x4 -> x0, waiting for transfers between devices: 46.1 us -> none
    reduce_scatter x1 -> x0, waiting for transfers between devices: 35.4 us -> none  [shards(): lax.psum_scatter(token_sums.reshape(vocabulary, branches, width), 'seq',...]
    dot_general x15 -> x0, matrix products: 27.3 us -> none  [the longest x2 3.76 us: complex_einsum(): jnp.einsum(formula, mat_imag, val_imag, precision=precise_mode)]
    all_gather x1 -> x0, waiting for transfers between devices: 24.8 us -> none  [shards(): full_table = lax.all_gather(own_table, 'seq', axis=3, tiled=True)]
    all_gather x1 -> x0, blocking collectives: 19.7 us -> none  [shards(): gathered = lax.all_gather(summed[:, :, None, :], 'red', axis=2, tiled=True)]
    all_to_all x1 -> x0, blocking collectives: 10.7 us -> none  [shards(): lax.all_to_all(results, 'seq', split_axis=0, concat_axis=2, tiled=True)]
    unnamed x28 -> x0, local copies, waits for them, and re-layouts: 9.24 us -> none
  transfers between devices with their start and end apart: 4 -> 0, of which waited for: 4 -> 0; matrix products, arithmetic and copies ran while one was open for 1% -> 0% of each run, Pallas kernels for 0% -> 0%
where the time goes in v3:
time: 53 us; the launch traced here: 52.8 us
  Pallas kernels  52.1 us (98%)
  between operations  0.64 us (1%)
    pallas_call x1, Pallas kernels, kernel_shards(): pl.pallas_call(functools.partial(main_kernel, devices, count, chunks, sca...  47.9 us
    pallas_call x1, Pallas kernels, kernel_shards(): pl.pallas_call(functools.partial(final_kernel, scale_factor), out_shape=(...  4.27 us

profile of v3, /device:TPU:0, one launch (start us, length us, event | category | flops | bytes accessed | tf_op | source)
XLA Modules:
  0.0 52.8 jit_solution(18197626990084646261)
XLA Ops:
  0.6 47.9 %hyena_exchange.1 = (f32[2,8,80,128]{3,2,1,0:T(8,128)}, f32[8,48,512]{2,1,0:T(8,128)}) custom-call(s32[1,128]{1,0:T(1,128)} %bitcast.5, bf16[512,1024]{1,0:T(8,128)(2,1)} %emb_ref.3, bf16[3,4,32,1024]{3,2,1,0:T(8,128)(2,1)} %bitcast.4, f32[128,256]{1,0:T(8,128)} %filt_ref.1, f32[128,256]{1,0:T(8,128)} %cot_ref.1, ...), custom_call_target="tpu_custom_call" | custom-call | tf_op jit(solution)/shard_map/hyena_exchange/pallas_call | solution.py:444
  48.5 4.3 %finish.1 = (f32[128,256]{1,0:T(8,128)}, f32[128,256]{1,0:T(8,128)}, bf16[3,128,256]{2,1,0:T(8,128)(2,1)}, f32[3,4,32,1024]{3,2,1,0:T(8,128)}) custom-call(bf16[512,1024]{1,0:T(8,128)(2,1)} %emb_ref.3, f32[2,8,80,128]{3,2,1,0:T(8,128)} %get-tuple-element.10.recv_ref, f32[8,48,512]{2,1,0:T(8,128)} %get-tuple-element.11.all_ref), custom_call_target="tpu_custom_call" | custom-call | tf_op jit(solution)/shard_map/finish/pallas_call | solution.py:472

commit v4 on v3

--- a/solution.py
+++ b/solution.py
@@ -12,7 +12,7 @@
 precise_mode = lax.Precision.HIGHEST
 MESH = pl.DeviceIdType.MESH
 VMEM = pl.BlockSpec(memory_space=pltpu.VMEM)
-CHUNKS = 2
+CHUNKS = 1
 NN = (((1,), (0,)), ((), ()))
 NT = (((1,), (1,)), ((), ()))
 

time: 53 us -> 46.5 us (0.88)
  Pallas kernels: 52.1 us -> 45.7 us
    pallas_call x1, Pallas kernels: 47.9 us -> 41.9 us  [kernel_shards(): pl.pallas_call(functools.partial(main_kernel, devices, count, chunks, sca...]
where the time goes in v4:
time: 46.5 us; the launch traced here: 46.4 us
  Pallas kernels  45.7 us (98%)
  between operations  0.64 us (1%)
    pallas_call x1, Pallas kernels, kernel_shards(): pl.pallas_call(functools.partial(main_kernel, devices, count, chunks, sca...  41.9 us
    pallas_call x1, Pallas kernels, kernel_shards(): pl.pallas_call(functools.partial(final_kernel, scale_factor), out_shape=(...  3.83 us

profile of v4, /device:TPU:0, one launch (start us, length us, event | category | flops | bytes accessed | tf_op | source)
XLA Modules:
  0.0 46.4 jit_solution(15830780718045189074)
XLA Ops:
  0.6 41.9 %hyena_exchange.1 = (f32[1,8,160,128]{3,2,1,0:T(8,128)}, f32[4,96,512]{2,1,0:T(8,128)}) custom-call(s32[1,128]{1,0:T(1,128)} %bitcast.5, bf16[512,1024]{1,0:T(8,128)(2,1)} %emb_ref.3, bf16[3,4,32,1024]{3,2,1,0:T(8,128)(2,1)} %bitcast.4, f32[128,256]{1,0:T(8,128)} %filt_ref.1, f32[128,256]{1,0:T(8,128)} %cot_ref.1, ...), custom_call_target="tpu_custom_call" | custom-call | tf_op jit(solution)/shard_map/hyena_exchange/pallas_call | solution.py:444
  42.5 3.8 %finish.1 = (f32[128,256]{1,0:T(8,128)}, f32[128,256]{1,0:T(8,128)}, bf16[3,128,256]{2,1,0:T(8,128)(2,1)}, f32[3,4,32,1024]{3,2,1,0:T(8,128)}) custom-call(bf16[512,1024]{1,0:T(8,128)(2,1)} %emb_ref.3, f32[1,8,160,128]{3,2,1,0:T(8,128)} %get-tuple-element.10.recv_ref, f32[4,96,512]{2,1,0:T(8,128)} %get-tuple-element.11.all_ref), custom_call_target="tpu_custom_call" | custom-call | tf_op jit(solution)/shard_map/finish/pallas_call | solution.py:472

commit v5 on v4

--- a/solution.py
+++ b/solution.py
@@ -194,6 +194,9 @@
             device_id_type=MESH,
         )
 
+    def place(chunk, branch):
+        return (chunk * branches + branch) * count
+
     def right(slot):
         return hop(part, from_left, slot, right_send, right_recv, above_spot)
 
@@ -210,68 +213,81 @@
         table = emb_ref[...]
         for group in range(count):
             rows = [wt_ref[b, group, chunk * sub : (chunk + 1) * sub] for b in range(branches)]
-            part[chunk * count + group] = dot(jnp.concatenate(rows, axis=0), table, NT)
+            product = dot(jnp.concatenate(rows, axis=0), table, NT)
+            for b in range(branches):
+                part[place(chunk, b) + group] = product[b * sub : (b + 1) * sub]
 
     def first_hops(chunk):
-        base = chunk * count
+        bases = [place(chunk, branch) for branch in range(branches)]
 
         @pl.when(spot == 0)
         def _():
             for goal in range(count - 1, 0, -1):
-                right(base + goal).start()
+                for base in bases:
+                    right(base + goal).start()
 
         @pl.when(spot == count - 1)
         def _():
             for goal in range(count - 1):
-                left(base + goal).start()
+                for base in bases:
+                    left(base + goal).start()
 
     def middle_hops(chunk):
-        base = chunk * count
         for tick in range(1, count - 1):
-            goal = count - 1 - (tick - spot)
-
-            @pl.when((spot > 0) & (tick >= spot) & (spot < goal))
-            def _():
-                right(base + goal).wait_recv()
-                part[base + goal] = part[base + goal] + from_left[base + goal]
-                right(base + goal).start()
-
-            other = tick - (count - 1 - spot)
-
-            @pl.when((spot < count - 1) & (other >= 0) & (spot > other))
-            def _():
-                left(base + other).wait_recv()
-                part[base + other] = part[base + other] + from_right[base + other]
-                left(base + other).start()
+            for branch in range(branches):
+                later_hop(place(chunk, branch), tick)
+
+    def later_hop(base, tick):
+        goal = count - 1 - (tick - spot)
+
+        @pl.when((spot > 0) & (tick >= spot) & (spot < goal))
+        def _():
+            right(base + goal).wait_recv()
+            part[base + goal] = part[base + goal] + from_left[base + goal]
+            right(base + goal).start()
+
+        other = tick - (count - 1 - spot)
+
+        @pl.when((spot < count - 1) & (other >= 0) & (spot > other))
+        def _():
+            left(base + other).wait_recv()
+            part[base + other] = part[base + other] + from_right[base + other]
+            left(base + other).start()
 
     def arrive(chunk):
-        slot = chunk * count + spot
-
-        @pl.when(spot > 0)
-        def _():
-            right(slot).wait_recv()
-            part[slot] = part[slot] + from_left[slot]
-
-        @pl.when(spot < count - 1)
-        def _():
-            left(slot).wait_recv()
-            part[slot] = part[slot] + from_right[slot]
-
-        return part[slot]
+        for branch in range(branches):
+            slot = place(chunk, branch) + spot
+
+            @pl.when(spot > 0)
+            def _():
+                right(slot).wait_recv()
+                part[slot] = part[slot] + from_left[slot]
+
+            @pl.when(spot < count - 1)
+            def _():
+                left(slot).wait_recv()
+                part[slot] = part[slot] + from_right[slot]
+
+        slots = [place(chunk, branch) + spot for branch in range(branches)]
+        return jnp.concatenate([part[slot] for slot in slots], axis=0)
 
     def share(chunk):
-        slot = chunk * count + spot
-
-        @pl.when(spot < count - 1)
-        def _():
-            up(slot).start()
-
-        @pl.when(spot > 0)
-        def _():
-            down(slot).start()
+        for branch in range(branches):
+            slot = place(chunk, branch) + spot
+
+            @pl.when(spot < count - 1)
+            def _():
+                up(slot).start()
+
+            @pl.when(spot > 0)
+            def _():
+                down(slot).start()
 
     def relay(chunk, step):
-        base = chunk * count
+        for branch in range(branches):
+            relay_block(place(chunk, branch), step)
+
+    def relay_block(base, step):
         below = spot - step
 
         @pl.when(below >= 0)
@@ -321,7 +337,9 @@
             sending[chunk, at, :sub] = queries[:, lanes] * conv
             sending[chunk, at, sub : 2 * sub] = results[at][2 * sub :] * scale_factor
             sending[chunk, at, 2 * sub :] = grads.astype(jnp.float32)
-        all_ref[chunk * count + spot] = dot(jnp.concatenate(rounded, axis=1), one_hot[...], NT)
+        sums = dot(jnp.concatenate(rounded, axis=1), one_hot[...], NT)
+        for b in range(branches):
+            all_ref[place(chunk, b) + spot] = sums[b * sub : (b + 1) * sub]
 
     filt_t = filt_ref[...].T
     cot_t = cot_ref[...].T
@@ -374,8 +392,7 @@
                 relay(chunk - 1, step)
     for step in range(1, count):
         relay(chunks - 1, step)
-    for chunk in range(chunks):
-        base = chunk * count
+    for base in range(0, chunks * branches * count, count):
         for goal in range(count):
             @pl.when(spot < goal)
             def _():
@@ -403,11 +420,12 @@
 def final_kernel(scale_factor, emb_ref, recv_ref, all_ref, out_ref, filt_ref, grads_ref, weight_ref):
     chunks, devices, rows, _ = recv_ref.shape
     sub = rows // 5
-    count = all_ref.shape[0] // chunks
+    count = all_ref.shape[0] // (chunks * 3)
     table = emb_ref[...]
     for chunk in range(chunks):
         for group in range(count):
-            product = dot_split(all_ref[chunk * count + group], table) * scale_factor
+            blocks = [all_ref[(chunk * 3 + branch) * count + group] for branch in range(3)]
+            product = dot_split(jnp.concatenate(blocks, axis=0), table) * scale_factor
             for branch in range(3):
                 weight_ref[branch, group, chunk * sub : (chunk + 1) * sub] = product[
                     branch * sub : (branch + 1) * sub
@@ -433,12 +451,12 @@
     _, branches, _, piece = proj_weight.shape
     scale_factor = float(tok_count * devices) ** (-0.5)
     chunks = CHUNKS
-    rows = branches * piece // chunks
+    rows = piece // chunks
     f32 = jnp.float32
     dma = pltpu.SemaphoreType.DMA
     weight_t = jnp.transpose(proj_weight, (1, 2, 3, 0))
     high, low = transform_tables(tok_count, devices)
-    block = (chunks * count, rows, vocabulary)
+    block = (chunks * branches * count, rows, vocabulary)
     message = (devices, 2 * piece + 8, tok_count)
     answer = (chunks, devices, 5 * piece // chunks, tok_count)
     received, all_sums = pl.pallas_call(
@@ -462,7 +480,7 @@
             dma((chunks * (devices - 1),)),
             dma((chunks * (devices - 1),)),
         ]
-        + [dma((chunks * count,))] * 8,
+        + [dma((chunks * branches * count,))] * 8,
         compiler_params=pltpu.CompilerParams(collective_id=0, has_side_effects=True),
         name="hyena_exchange",
     )(

time: 46.5 us -> 45.5 us (0.978)
  Pallas kernels: 45.7 us -> 44.7 us
    pallas_call x1, Pallas kernels: 41.9 us -> 40.9 us  [kernel_shards(): pl.pallas_call(functools.partial(main_kernel, devices, count, chunks, sca...]
where the time goes in v5:
time: 45.5 us; the launch traced here: 45.3 us
  Pallas kernels  44.7 us (98%)
  between operations  0.64 us (1%)
    pallas_call x1, Pallas kernels, kernel_shards(): pl.pallas_call(functools.partial(main_kernel, devices, count, chunks, sca...  40.9 us
    pallas_call x1, Pallas kernels, kernel_shards(): pl.pallas_call(functools.partial(final_kernel, scale_factor), out_shape=(...  3.83 us

profile of v5, /device:TPU:0, one launch (start us, length us, event | category | flops | bytes accessed | tf_op | source)
XLA Modules:
  0.0 45.3 jit_solution(120432655009519807)
XLA Ops:
  0.6 40.9 %hyena_exchange.1 = (f32[1,8,160,128]{3,2,1,0:T(8,128)}, f32[12,32,512]{2,1,0:T(8,128)}) custom-call(s32[1,128]{1,0:T(1,128)} %bitcast.5, bf16[512,1024]{1,0:T(8,128)(2,1)} %emb_ref.3, bf16[3,4,32,1024]{3,2,1,0:T(8,128)(2,1)} %bitcast.4, f32[128,256]{1,0:T(8,128)} %filt_ref.1, f32[128,256]{1,0:T(8,128)} %cot_ref.1, ...), custom_call_target="tpu_custom_call" | custom-call | tf_op jit(solution)/shard_map/hyena_exchange/pallas_call | solution.py:462
  41.5 3.8 %finish.1 = (f32[128,256]{1,0:T(8,128)}, f32[128,256]{1,0:T(8,128)}, bf16[3,128,256]{2,1,0:T(8,128)(2,1)}, f32[3,4,32,1024]{3,2,1,0:T(8,128)}) custom-call(bf16[512,1024]{1,0:T(8,128)(2,1)} %emb_ref.3, f32[1,8,160,128]{3,2,1,0:T(8,128)} %get-tuple-element.10.recv_ref, f32[12,32,512]{2,1,0:T(8,128)} %get-tuple-element.11.all_ref), custom_call_target="tpu_custom_call" | custom-call | tf_op jit(solution)/shard_map/finish/pallas_call | solution.py:490

commit v6 on v5

--- a/solution.py
+++ b/solution.py
@@ -420,16 +420,14 @@
 def final_kernel(scale_factor, emb_ref, recv_ref, all_ref, out_ref, filt_ref, grads_ref, weight_ref):
     chunks, devices, rows, _ = recv_ref.shape
     sub = rows // 5
-    count = all_ref.shape[0] // (chunks * 3)
     table = emb_ref[...]
     for chunk in range(chunks):
-        for group in range(count):
-            blocks = [all_ref[(chunk * 3 + branch) * count + group] for branch in range(3)]
-            product = dot_split(jnp.concatenate(blocks, axis=0), table) * scale_factor
-            for branch in range(3):
-                weight_ref[branch, group, chunk * sub : (chunk + 1) * sub] = product[
-                    branch * sub : (branch + 1) * sub
-                ]
+        blocks = [all_ref[chunk * 3 + branch, 0] for branch in range(3)]
+        product = dot_split(jnp.concatenate(blocks, axis=0), table) * scale_factor
+        for branch in range(3):
+            weight_ref[branch, 0, chunk * sub : (chunk + 1) * sub] = product[
+                branch * sub : (branch + 1) * sub
+            ]
 
     def positions(at):
         parts = [
@@ -439,10 +437,12 @@
         ]
         return jnp.concatenate(parts, axis=0).T
 
-    out_ref[...] = positions(0)
-    filt_ref[...] = positions(1)
-    for branch in range(3):
-        grads_ref[branch] = positions(2 + branch).astype(jnp.bfloat16)
+    @pl.when(pl.program_id(0) == 0)
+    def _():
+        out_ref[...] = positions(0)
+        filt_ref[...] = positions(1)
+        for branch in range(3):
+            grads_ref[branch] = positions(2 + branch).astype(jnp.bfloat16)
 
 
 def kernel_shards(devices, count, token_ids, embedding, proj_weight, filters, cotangent):
@@ -495,10 +495,20 @@
             jax.ShapeDtypeStruct((branches, tok_count, width), jnp.bfloat16),
             jax.ShapeDtypeStruct((branches, count, piece, depth), f32),
         ),
-        in_specs=[VMEM] * 3,
-        out_specs=(VMEM,) * 4,
+        grid=(count,),
+        in_specs=[
+            pl.BlockSpec(embedding.shape, lambda group: (0, 0)),
+            pl.BlockSpec(answer, lambda group: (0, 0, 0, 0)),
+            pl.BlockSpec((branches * chunks, 1, rows, vocabulary), lambda group: (0, group, 0, 0)),
+        ],
+        out_specs=(
+            pl.BlockSpec((tok_count, width), lambda group: (0, 0)),
+            pl.BlockSpec((tok_count, width), lambda group: (0, 0)),
+            pl.BlockSpec((branches, tok_count, width), lambda group: (0, 0, 0)),
+            pl.BlockSpec((branches, 1, piece, depth), lambda group: (0, group, 0, 0)),
+        ),
         name="finish",
-    )(embedding, received, all_sums)
+    )(embedding, received, all_sums.reshape(branches * chunks, count, rows, vocabulary))
     return (
         output,
         filter_grad,

time: 45.5 us -> 46.8 us (1.029)
  Pallas kernels: 44.7 us -> 46 us
    pallas_call x1, Pallas kernels: 3.83 us -> 5.1 us  [kernel_shards(): pl.pallas_call(functools.partial(final_kernel, scale_factor), out_shape=(...]
where the time goes in v6:
time: 46.8 us; the launch traced here: 46.6 us
  Pallas kernels  46 us (98%)
  between operations  0.64 us (1%)
    pallas_call x1, Pallas kernels, kernel_shards(): pl.pallas_call(functools.partial(main_kernel, devices, count, chunks, sca...  40.9 us
    pallas_call x1, Pallas kernels, kernel_shards(): pl.pallas_call(functools.partial(final_kernel, scale_factor), out_shape=(...  5.1 us

profile of v6, /device:TPU:0, one launch (start us, length us, event | category | flops | bytes accessed | tf_op | source)
XLA Modules:
  0.0 46.6 jit_solution(4531318903294297560)
XLA Ops:
  0.6 40.9 %hyena_exchange.1 = (f32[1,8,160,128]{3,2,1,0:T(8,128)}, f32[12,32,512]{2,1,0:T(8,128)}) custom-call(s32[1,128]{1,0:T(1,128)} %bitcast.7, bf16[512,1024]{1,0:T(8,128)(2,1)} %emb_ref.3, bf16[3,4,32,1024]{3,2,1,0:T(8,128)(2,1)} %bitcast.5, f32[128,256]{1,0:T(8,128)} %filt_ref.1, f32[128,256]{1,0:T(8,128)} %cot_ref.1, ...), custom_call_target="tpu_custom_call" | custom-call | tf_op jit(solution)/shard_map/hyena_exchange/pallas_call | solution.py:462
  41.5 5.1 %finish.1 = (f32[128,256]{1,0:T(8,128)}, f32[128,256]{1,0:T(8,128)}, bf16[3,128,256]{2,1,0:T(8,128)(2,1)}, f32[3,4,32,1024]{3,2,1,0:T(8,128)}) custom-call(bf16[512,1024]{1,0:T(8,128)(2,1)} %emb_ref.3, f32[1,8,160,128]{3,2,1,0:T(8,128)} %get-tuple-element.10.recv_ref, f32[3,4,32,512]{3,2,1,0:T(8,128)} %bitcast.6), custom_call_target="tpu_custom_call" | custom-call | tf_op jit(solution)/shard_map/finish/pallas_call | solution.py:490
